TPU v7x, 32 devices: a whole 2x2x4 slice. The times are simulated.
32 devices in a mesh: blk: 8 (over y, x, core), rows: 4 (over z).
Axes of the slice: x: 2, y: 2, z: 4, core: 2. Of those that a mesh axis runs over, the one named last changes fastest.
Arguments:
- sens_tiles: bfloat16 [2048, 512, 128], P('blk', 'rows'), may hold values from -1 to 1
- start_basis: bfloat16 [64, 32768], P(None, 'blk'), may hold values from -6 to 6
- row_blocks: int32 [2048, 4], P('blk', 'rows'), may hold values from 0 to 7, as said below
- col_blocks: int32 [2048, 4], P('blk', 'rows'), may hold values from 0 to 31, as said below
- live_counts: int32 [8, 4], P('blk', 'rows'), may hold values from 64 to 256, as said below
Outputs:
- orthonormal: float32 [4, 64, 32768], P(None, None, ('blk', 'rows'))
Inputs may be any that keep to these rules, and one draw needn't show every extreme that they name: Within one device the pairs (row_blocks, col_blocks) of its 256 slots are distinct. Within one device the pairs (row_blocks, col_blocks) of its 256 slots are distinct. Slots 0 to live_counts - 1 of a device hold its tiles; some device has all 256 slots live.
All inputs are finite; a program needn't handle non-finite values.
Results may differ from a plain program's by a relative error of at most 0.012.
The roundings to bfloat16 on the way count: a program that leaves them out, or rounds other values in their place, can miss the bound.
Values may be sent and summed in bfloat16 or wider, within the bound.
A program may use at most 128 MiB of HBM per device.

v0:
```python
import jax
import jax.numpy as jnp
from jax import lax
from jax.sharding import PartitionSpec as P

RB = 8
CB = 32
ITERS = 4


def apply_forward(sens_tiles, basis_now, col_slots, row_onehot):
    vectors = basis_now.shape[0]
    tile_size = sens_tiles.shape[2]
    picked = jnp.take(basis_now.reshape(vectors, CB, tile_size), col_slots, axis=1)
    products = jnp.einsum("kst,sit->ksi", picked, sens_tiles, preferred_element_type=jnp.float32)
    summed = jnp.einsum("ksi,rs->kri", products, row_onehot, precision=lax.Precision.HIGHEST)
    return summed.reshape(vectors, RB * tile_size)


def apply_backward(sens_tiles, image_half, row_slots, col_onehot):
    vectors = image_half.shape[0]
    tile_size = sens_tiles.shape[2]
    picked = jnp.take(image_half.reshape(vectors, RB, tile_size), row_slots, axis=1)
    products = jnp.einsum("ksi,sij->ksj", picked, sens_tiles, preferred_element_type=jnp.float32)
    summed = jnp.einsum("ksj,cs->kcj", products, col_onehot, precision=lax.Precision.HIGHEST)
    return summed.reshape(vectors, CB * tile_size)


def factor_whole(current, total):
    local_gram = jnp.dot(current, current.T, precision=lax.Precision.HIGHEST)
    gram = lax.psum(local_gram, "blk") / total
    lower = jnp.linalg.cholesky(gram)
    return jax.scipy.linalg.solve_triangular(lower, current, lower=True)


def local(sens_tiles, start_basis, row_blocks, col_blocks, live_counts):
    row_slots = row_blocks[:, 0]
    col_slots = col_blocks[:, 0]
    count_live = live_counts[0, 0]
    slot_total = sens_tiles.shape[0]
    tile_size = sens_tiles.shape[2]
    live = jnp.arange(slot_total) < count_live
    row_onehot = ((row_slots[None, :] == jnp.arange(RB)[:, None]) & live[None, :]).astype(
        jnp.float32
    )
    col_onehot = ((col_slots[None, :] == jnp.arange(CB)[:, None]) & live[None, :]).astype(
        jnp.float32
    )
    total = float(CB * tile_size * lax.axis_size("blk"))
    own_width = CB * tile_size // lax.axis_size("rows")
    basis_now = start_basis
    results = []
    for iteration in range(ITERS):
        partial_image = apply_forward(sens_tiles, basis_now, col_slots, row_onehot)
        image = lax.psum(partial_image, "blk")
        image_half = image.astype(jnp.bfloat16)
        partial_hessian = apply_backward(sens_tiles, image_half, row_slots, col_onehot)
        hessian = lax.psum(partial_hessian, "rows")
        whole_result = factor_whole(hessian, total)
        basis_now = whole_result.astype(jnp.bfloat16)
        result = lax.dynamic_slice_in_dim(
            whole_result, lax.axis_index("rows") * own_width, own_width, 1
        )
        results.append(result)
    return jnp.stack(results, axis=0)


def solution(mesh):
    in_specs = (
        P("blk", "rows", None),
        P(None, "blk"),
        P("blk", "rows"),
        P("blk", "rows"),
        P("blk", "rows"),
    )
    out_specs = P(None, None, ("blk", "rows"))
    return jax.shard_map(local, mesh=mesh, in_specs=in_specs, out_specs=out_specs, check_vma=False)
```

profile of v0, /device:TPU:0, one launch (start us, length us, event | category | flops | bytes accessed | tf_op | source)
XLA Modules:
  0.0 653.3 jit_solution(9419659961309902612)
XLA Ops:
  9.5 3.0 gather_fusion
  12.5 10.4 %fusion.48 = f32[64,256,128]{2,0,1:T(8,128)S(1)} fusion(bf16[256,128,128]{2,1,0:T(8,128)(2,1)} %param.12, bf16[256,64,128]{2,1,0:T(8,128)(2,1)} %gather_fusion, pred[256]{0:T(512)(128)(4,1)S(1)} %get-tuple-element.8), kind=kOutput, calls=%fused_computation.56 | convolution fusion | flops 538968064 | bytes 20971776 | tf_op jit(solution)/shard_map/kst,sit->ksi/dot_general | solution.py:15
  22.9 7.5 %fusion.14 = f32[8,64,128]{2,0,1:T(8,128)S(1)} fusion(f32[64,256,128]{2,0,1:T(8,128)S(1)} %fusion.48, s32[256]{0:T(256)S(1)} %bitcast.242, pred[256]{0:T(512)(128)(4,1)S(1)} %iota_compare_fusion.4), kind=kOutput, calls=%fused_computation.22 | convolution fusion | flops 201330688 | bytes 8652032 | tf_op jit(solution)/shard_map/ksi,rs->kri/dot_general | solution.py:16
  30.8 28.4 %all-reduce.16 = bf16[64,1024]{1,0:T(8,128)(2,1)S(1)} all-reduce(f32[64,1024]{1,0:T(8,128)S(1)} %bitcast.236), channel_id=1, replica_groups=mesh['blk'=8,'rows'=4] {'blk'}, use_global_device_ids=true, to_apply=%region_0.0 | all-reduce | flops 65536 | bytes 393216 | tf_op jit(solution)/shard_map/psum | solution.py:55
  59.3 3.0 gather_fusion.1
  62.3 7.0 %fusion.51 = f32[64,256,128]{2,0,1:T(8,128)S(1)} fusion(bf16[256,128,128]{2,1,0:T(8,128)(2,1)} %param.12, bf16[256,64,128]{2,1,0:T(8,128)(2,1)} %gather_fusion.1, pred[256]{0:T(512)(128)(4,1)S(1)} %get-tuple-element.6), kind=kOutput, calls=%fused_computation.57 | convolution fusion | flops 538968064 | bytes 20971776 | tf_op jit(solution)/shard_map/ksi,sij->ksj/dot_general | solution.py:24
  69.4 7.7 %fusion.12 = f32[32,64,128]{2,0,1:T(8,128)S(1)} fusion(f32[64,256,128]{2,0,1:T(8,128)S(1)} %fusion.51, s32[256]{0:T(256)S(1)} %bitcast.248, pred[256]{0:T(512)(128)(4,1)S(1)} %iota_compare_fusion.4), kind=kOutput, calls=%fused_computation.20 | convolution fusion | flops 805322752 | bytes 9438464 | tf_op jit(solution)/shard_map/ksj,cs->kcj/dot_general | solution.py:25
  78.7 51.6 %all-reduce.9.cloned.1.call-done = f32[64,4096]{1,0:T(8,128)} async-done(((f32[64,4096]{1,0:T(8,128)}), f32[64,4096]{1,0:T(8,128)}) %all-reduce.9.cloned.1.call-update) | async-done | bytes 1048592 | tf_op jit(solution)/shard_map/psum | solution.py:58
  130.3 2.5 fusion.116
  132.8 24.3 %psum.86 = f32[64,64]{0,1:T(8,128)S(1)} all-reduce(f32[64,64]{0,1:T(8,128)S(1)} %fusion.116), channel_id=1, replica_groups=mesh['blk'=8,'rows'=4] {'blk'}, use_global_device_ids=true, to_apply=%region_2.0 | all-reduce | flops 4096 | bytes 32768 | tf_op jit(solution)/shard_map/psum | solution.py:31
  157.2 5.8 cholesky.74
  164.4 4.9 custom-call.8
  172.7 3.0 gather_fusion.2
  175.7 10.4 %fusion.54 = f32[64,256,128]{2,0,1:T(8,128)S(1)} fusion(bf16[256,128,128]{2,1,0:T(8,128)(2,1)} %param.12, bf16[256,64,128]{2,1,0:T(8,128)(2,1)} %gather_fusion.2, pred[256]{0:T(512)(128)(4,1)S(1)} %get-tuple-element.8), kind=kOutput, calls=%fused_computation.58 | convolution fusion | flops 538968064 | bytes 20971776 | tf_op jit(solution)/shard_map/kst,sit->ksi/dot_general | solution.py:15
  186.1 7.9 %fusion.10 = f32[8,64,128]{2,0,1:T(8,128)S(1)} fusion(f32[64,256,128]{2,0,1:T(8,128)S(1)} %fusion.54, s32[256]{0:T(256)S(1)} %bitcast.243, pred[256]{0:T(512)(128)(4,1)S(1)} %iota_compare_fusion.4), kind=kOutput, calls=%fused_computation.18 | convolution fusion | flops 201330688 | bytes 8652032 | tf_op jit(solution)/shard_map/ksi,rs->kri/dot_general | solution.py:16
  194.0 25.3 %all-reduce.17 = bf16[64,1024]{1,0:T(8,128)(2,1)S(1)} all-reduce(f32[64,1024]{1,0:T(8,128)S(1)} %bitcast.237), channel_id=1, replica_groups=mesh['blk'=8,'rows'=4] {'blk'}, use_global_device_ids=true, to_apply=%region_5.10 | all-reduce | flops 65536 | bytes 393216 | tf_op jit(solution)/shard_map/psum | solution.py:55
  219.3 3.0 gather_fusion.3
  222.3 7.0 %fusion.57 = f32[64,256,128]{2,0,1:T(8,128)S(1)} fusion(bf16[256,128,128]{2,1,0:T(8,128)(2,1)} %param.12, bf16[256,64,128]{2,1,0:T(8,128)(2,1)} %gather_fusion.3, pred[256]{0:T(512)(128)(4,1)S(1)} %get-tuple-element.6), kind=kOutput, calls=%fused_computation.59 | convolution fusion | flops 538968064 | bytes 20971776 | tf_op jit(solution)/shard_map/ksi,sij->ksj/dot_general | solution.py:24
  229.4 7.7 %fusion.8 = f32[32,64,128]{2,0,1:T(8,128)S(1)} fusion(f32[64,256,128]{2,0,1:T(8,128)S(1)} %fusion.57, s32[256]{0:T(256)S(1)} %bitcast.249, pred[256]{0:T(512)(128)(4,1)S(1)} %iota_compare_fusion.4), kind=kOutput, calls=%fused_computation.16 | convolution fusion | flops 805322752 | bytes 9438464 | tf_op jit(solution)/shard_map/ksj,cs->kcj/dot_general | solution.py:25
  238.8 49.5 %all-reduce.11.cloned.1.call-done = f32[64,4096]{1,0:T(8,128)} async-done(((f32[64,4096]{1,0:T(8,128)}), f32[64,4096]{1,0:T(8,128)}) %all-reduce.11.cloned.1.call-update) | async-done | bytes 1048592 | tf_op jit(solution)/shard_map/psum | solution.py:58
  288.2 2.5 fusion.117
  290.7 24.3 %psum.89 = f32[64,64]{0,1:T(8,128)S(1)} all-reduce(f32[64,64]{0,1:T(8,128)S(1)} %fusion.117), channel_id=1, replica_groups=mesh['blk'=8,'rows'=4] {'blk'}, use_global_device_ids=true, to_apply=%region_7.12 | all-reduce | flops 4096 | bytes 32768 | tf_op jit(solution)/shard_map/psum | solution.py:31
  315.1 5.8 cholesky.85
  322.3 4.9 custom-call.9
  330.6 3.0 gather_fusion.4
  333.6 10.4 %fusion.60 = f32[64,256,128]{2,0,1:T(8,128)S(1)} fusion(bf16[256,128,128]{2,1,0:T(8,128)(2,1)} %param.12, bf16[256,64,128]{2,1,0:T(8,128)(2,1)} %gather_fusion.4, pred[256]{0:T(512)(128)(4,1)S(1)} %get-tuple-element.8), kind=kOutput, calls=%fused_computation.60 | convolution fusion | flops 538968064 | bytes 20971776 | tf_op jit(solution)/shard_map/kst,sit->ksi/dot_general | solution.py:15
  344.0 7.9 %fusion.6 = f32[8,64,128]{2,0,1:T(8,128)S(1)} fusion(f32[64,256,128]{2,0,1:T(8,128)S(1)} %fusion.60, s32[256]{0:T(256)S(1)} %bitcast.244, pred[256]{0:T(512)(128)(4,1)S(1)} %iota_compare_fusion.4), kind=kOutput, calls=%fused_computation.14 | convolution fusion | flops 201330688 | bytes 8652032 | tf_op jit(solution)/shard_map/ksi,rs->kri/dot_general | solution.py:16
  352.0 25.3 %all-reduce.18 = bf16[64,1024]{1,0:T(8,128)(2,1)S(1)} all-reduce(f32[64,1024]{1,0:T(8,128)S(1)} %bitcast.238), channel_id=1, replica_groups=mesh['blk'=8,'rows'=4] {'blk'}, use_global_device_ids=true, to_apply=%region_8.13 | all-reduce | flops 65536 | bytes 393216 | tf_op jit(solution)/shard_map/psum | solution.py:55
  377.3 3.0 gather_fusion.5
  380.3 7.0 %fusion.63 = f32[64,256,128]{2,0,1:T(8,128)S(1)} fusion(bf16[256,128,128]{2,1,0:T(8,128)(2,1)} %param.12, bf16[256,64,128]{2,1,0:T(8,128)(2,1)} %gather_fusion.5, pred[256]{0:T(512)(128)(4,1)S(1)} %get-tuple-element.6), kind=kOutput, calls=%fused_computation.61 | convolution fusion | flops 538968064 | bytes 20971776 | tf_op jit(solution)/shard_map/ksi,sij->ksj/dot_general | solution.py:24
  387.3 7.7 %fusion.4 = f32[32,64,128]{2,0,1:T(8,128)S(1)} fusion(f32[64,256,128]{2,0,1:T(8,128)S(1)} %fusion.63, s32[256]{0:T(256)S(1)} %bitcast.250, pred[256]{0:T(512)(128)(4,1)S(1)} %iota_compare_fusion.4), kind=kOutput, calls=%fused_computation.12 | convolution fusion | flops 805322752 | bytes 9438464 | tf_op jit(solution)/shard_map/ksj,cs->kcj/dot_general | solution.py:25
  396.7 49.5 %all-reduce.13.cloned.1.call-done = f32[64,4096]{1,0:T(8,128)} async-done(((f32[64,4096]{1,0:T(8,128)}), f32[64,4096]{1,0:T(8,128)}) %all-reduce.13.cloned.1.call-update) | async-done | bytes 1048592 | tf_op jit(solution)/shard_map/psum | solution.py:58
  446.2 2.5 fusion.118
  448.7 24.2 %psum.92 = f32[64,64]{0,1:T(8,128)S(1)} all-reduce(f32[64,64]{0,1:T(8,128)S(1)} %fusion.118), channel_id=1, replica_groups=mesh['blk'=8,'rows'=4] {'blk'}, use_global_device_ids=true, to_apply=%region_10.15 | all-reduce | flops 4096 | bytes 32768 | tf_op jit(solution)/shard_map/psum | solution.py:31
  473.1 5.8 cholesky.96
  480.2 4.9 custom-call.10
  488.5 3.0 gather_fusion.6
  491.6 10.4 %fusion.66 = f32[64,256,128]{2,0,1:T(8,128)S(1)} fusion(bf16[256,128,128]{2,1,0:T(8,128)(2,1)} %param.12, bf16[256,64,128]{2,1,0:T(8,128)(2,1)} %gather_fusion.6, pred[256]{0:T(512)(128)(4,1)S(1)} %get-tuple-element.8), kind=kOutput, calls=%fused_computation.62 | convolution fusion | flops 538968064 | bytes 20971776 | tf_op jit(solution)/shard_map/kst,sit->ksi/dot_general | solution.py:15
  501.9 7.7 %fusion.2 = f32[8,64,128]{2,0,1:T(8,128)S(1)} fusion(f32[64,256,128]{2,0,1:T(8,128)S(1)} %fusion.66, s32[256]{0:T(256)S(1)} %bitcast.245, pred[256]{0:T(512)(128)(4,1)S(1)} %iota_compare_fusion.4), kind=kOutput, calls=%fused_computation.10 | convolution fusion | flops 201330688 | bytes 8652032 | tf_op jit(solution)/shard_map/ksi,rs->kri/dot_general | solution.py:16
  509.7 25.3 %all-reduce.19 = bf16[64,1024]{1,0:T(8,128)(2,1)S(1)} all-reduce(f32[64,1024]{1,0:T(8,128)S(1)} %bitcast.239), channel_id=1, replica_groups=mesh['blk'=8,'rows'=4] {'blk'}, use_global_device_ids=true, to_apply=%region_11.16 | all-reduce | flops 65536 | bytes 393216 | tf_op jit(solution)/shard_map/psum | solution.py:55
  535.0 3.0 gather_fusion.7
  538.0 7.0 %fusion.69 = f32[64,256,128]{2,0,1:T(8,128)S(1)} fusion(bf16[256,128,128]{2,1,0:T(8,128)(2,1)} %param.12, bf16[256,64,128]{2,1,0:T(8,128)(2,1)} %gather_fusion.7, pred[256]{0:T(512)(128)(4,1)S(1)} %get-tuple-element.6), kind=kOutput, calls=%fused_computation.63 | convolution fusion | flops 538968064 | bytes 20971776 | tf_op jit(solution)/shard_map/ksi,sij->ksj/dot_general | solution.py:24
  545.1 7.7 %fusion = f32[32,64,128]{2,0,1:T(8,128)S(1)} fusion(f32[64,256,128]{2,0,1:T(8,128)S(1)} %fusion.69, s32[256]{0:T(256)S(1)} %bitcast.251, pred[256]{0:T(512)(128)(4,1)S(1)} %iota_compare_fusion.4), kind=kOutput, calls=%fused_computation.8 | convolution fusion | flops 805322752 | bytes 9438464 | tf_op jit(solution)/shard_map/ksj,cs->kcj/dot_general | solution.py:25
  557.4 46.5 %all-reduce.15.cloned.1.call-done = f32[64,4096]{1,0:T(8,128)} async-done(((f32[64,4096]{1,0:T(8,128)}), f32[64,4096]{1,0:T(8,128)}) %all-reduce.15.cloned.1.call-update) | async-done | bytes 1048592 | tf_op jit(solution)/shard_map/psum | solution.py:58
  603.9 2.8 fusion.119
  606.7 24.1 %psum.95 = f32[64,64]{0,1:T(8,128)S(1)} all-reduce(f32[64,64]{0,1:T(8,128)S(1)} %fusion.119), channel_id=1, replica_groups=mesh['blk'=8,'rows'=4] {'blk'}, use_global_device_ids=true, to_apply=%region_13.18 | all-reduce | flops 4096 | bytes 32768 | tf_op jit(solution)/shard_map/psum | solution.py:31
  630.9 5.8 cholesky.107
  638.1 4.9 custom-call.11
  (77 shorter events, 31.5 us)
Async XLA Ops:
  6.5 2.8 copy-start
  6.5 123.8 %all-reduce.9.cloned.1.call-start = ((), (), s32[]{:S(2)}) async-start(), calls=%async_computation | async-start | bytes 2097152 | tf_op jit(solution)/shard_map/psum | solution.py:58
  12.5 10.4 %copy-start.5 = (s32[256,1]{0,1:T(1,128)S(1)}, s32[256,1]{0,1:T(1,128)}, u32[]{:S(2)}) copy-start(s32[256,1]{0,1:T(1,128)} %param.14) | copy-start | bytes 3076
  62.3 7.0 %copy-start.6 = (s32[256,1]{0,1:T(1,128)S(1)}, s32[256,1]{0,1:T(1,128)}, u32[]{:S(2)}) copy-start(s32[256,1]{0,1:T(1,128)} %param.15) | copy-start | bytes 3076
  78.7 209.5 %all-reduce.11.cloned.1.call-start = ((), (), s32[]{:S(2)}) async-start(), calls=%async_computation.1 | async-start | bytes 2097152 | tf_op jit(solution)/shard_map/psum | solution.py:58
  171.6 1.0 copy-start.2
  238.7 207.5 %all-reduce.13.cloned.1.call-start = ((), (), s32[]{:S(2)}) async-start(), calls=%async_computation.2 | async-start | bytes 2097152 | tf_op jit(solution)/shard_map/psum | solution.py:58
  329.5 1.0 copy-start.3
  396.7 207.2 %all-reduce.15.cloned.1.call-start = ((), (), s32[]{:S(2)}) async-start(), calls=%async_computation.3 | async-start | bytes 2097152 | tf_op jit(solution)/shard_map/psum | solution.py:58
  487.4 1.0 copy-start.4
  554.4 91.9 %copy-start.1 = (bf16[64,4096]{1,0:T(8,128)(2,1)S(1)}, bf16[64,4096]{1,0:T(8,128)(2,1)}, u32[]{:S(2)}) copy-start(bf16[64,4096]{1,0:T(8,128)(2,1)} %param.13) | copy-start | bytes 1572868
Sparse Core Ops, SparseCore 0:
  78.8 51.4 all-reduce.8
  238.8 49.3 all-reduce.10
  396.8 49.3 all-reduce.12
  554.5 49.3 all-reduce.14
where the time goes:
time: 663 us; the launch traced here: 653 us
  blocking collectives  201 us (30%)
  waiting for transfers between devices  197 us (30%)
  matrix products  151 us (23%)
  other arithmetic  51.9 us (8%)
  local copies, waits for them, and re-layouts  37.5 us (6%)
  between operations  14.7 us (2%)
    psum x4, waiting for transfers between devices, local(): hessian = lax.psum(partial_hessian, 'rows')  197 us
    psum x4, blocking collectives, local(): image = lax.psum(partial_image, 'blk')  104 us
    psum x4, blocking collectives, factor_whole(): gram = lax.psum(local_gram, 'blk') / total  96.9 us
    dot_general x4, matrix products, apply_forward(): jnp.einsum('kst,sit->ksi', picked, sens_tiles, preferred_element_type=jnp...  41.5 us
    dot_general x4, matrix products, apply_forward(): jnp.einsum('ksi,rs->kri', products, row_onehot, precision=lax.Precision.H...  31 us
    dot_general x4, matrix products, apply_backward(): jnp.einsum('ksj,cs->kcj', products, col_onehot, precision=lax.Precision.H...  30.9 us
    dot_general x4, matrix products, apply_backward(): jnp.einsum('ksi,sij->ksj', picked, sens_tiles, preferred_element_type=jnp...  28.1 us
    another operation x12, other arithmetic, factor_whole(): lower = jnp.linalg.cholesky(gram)  26.1 us
  transfers between devices with their start and end apart: 4, of which 4 were waited for; matrix products, arithmetic and copies ran while one was open for 0% of the time, Pallas kernels for 0%

commit v1 on v0

v1 whole, which is shorter than its diff:
```python
import functools

import jax
import jax.numpy as jnp
from jax import lax
from jax.experimental import pallas as pl
from jax.experimental.pallas import tpu as pltpu
from jax.sharding import PartitionSpec as P

RB = 8
CB = 32
ITERS = 4
MESH = pl.DeviceIdType.MESH
F32 = jnp.float32
BF16 = jnp.bfloat16
HIGHEST = lax.Precision.HIGHEST


def aligned(index, width):
    return pl.ds(pl.multiple_of(index * width, width), width)


def inverse_factor(gram):
    size = gram.shape[0]
    row_id = lax.broadcasted_iota(jnp.int32, (size, size), 0)
    lane_id = lax.broadcasted_iota(jnp.int32, (size, size), 1)
    eye = (row_id == lane_id).astype(F32)
    whole = jnp.concatenate([gram, eye], axis=1)
    step = 8
    blocks = [whole[b * step : (b + 1) * step, :] for b in range(size // step)]
    sub_id = lax.broadcasted_iota(jnp.int32, (step, 2 * size), 0)
    for j in range(size):
        home, within = divmod(j, step)
        row = blocks[home][within : within + 1, :]
        scaled = row / row[:, j : j + 1]
        for b in range(home, size // step):
            update = blocks[b][:, j : j + 1] * scaled
            if b == home:
                update = jnp.where(sub_id > within, update, 0.0)
            blocks[b] = blocks[b] - update
    whole = jnp.concatenate(blocks, axis=0)
    pivots = jnp.sum(whole[:, :size] * eye, axis=1, keepdims=True)
    return whole[:, size:] * (1.0 / jnp.sqrt(pivots))


def kernel(
    n,
    m,
    total,
    inv_ref,
    tiles_hbm,
    start_ref,
    out_ref,
    tiles,
    dense,
    basis,
    part,
    rs_buf,
    half_own,
    half,
    hess_own,
    up_out,
    up_buf,
    down_out,
    down_buf,
    gram_own,
    gram_rows,
    gram_line,
    gram_blk,
    load_sem,
    rs_send,
    rs_recv,
    ag_send,
    ag_recv,
    up_send,
    up_recv,
    down_send,
    down_recv,
    gr_send,
    gr_recv,
    gb_send,
    gb_recv,
    bu_send,
    bu_recv,
    bd_send,
    bd_recv,
):
    slots = tiles_hbm.shape[0]
    tile = tiles_hbm.shape[1]
    vectors = start_ref.shape[0]
    data = RB * tile
    cells = start_ref.shape[1]
    width = cells // m
    owners = min(n, RB)
    span = data // owners
    b = lax.axis_index("blk")
    z = lax.axis_index("rows")

    load = pltpu.make_async_copy(tiles_hbm, tiles.at[pl.ds(0, slots)], load_sem)
    load.start()

    barrier = pltpu.get_barrier_semaphore()

    @pl.loop(1, n)
    def _(d):
        pl.semaphore_signal(
            barrier, inc=1, device_id={"blk": lax.rem(b + d, n)}, device_id_type=MESH
        )

    @pl.loop(1, m)
    def _(d):
        pl.semaphore_signal(
            barrier, inc=1, device_id={"rows": lax.rem(z + d, m)}, device_id_type=MESH
        )

    tiles[slots] = jnp.zeros((tile, tile), BF16)
    basis[...] = start_ref[...]
    load.wait()

    @pl.loop(0, RB)
    def _(r):
        @pl.loop(0, CB)
        def _(c):
            dense[aligned(r, tile), aligned(c, tile)] = tiles[inv_ref[r * CB + c]]

    pl.semaphore_wait(barrier, n - 1 + m - 1)

    def copy(src, dst, send_sem, recv_sem, where):
        return pltpu.make_async_remote_copy(
            src_ref=src,
            dst_ref=dst,
            send_sem=send_sem,
            recv_sem=recv_sem,
            device_id=where,
            device_id_type=MESH,
        )

    def rs_copy(dest, slot):
        return copy(
            part.at[:, aligned(dest, span)],
            rs_buf.at[slot],
            rs_send.at[dest],
            rs_recv.at[slot],
            {"blk": dest},
        )

    def ag_copy(dest, chunk):
        return copy(
            half_own,
            half.at[:, aligned(chunk, span)],
            ag_send.at[dest],
            ag_recv.at[chunk],
            {"blk": dest},
        )

    def up_copy(c):
        return copy(up_out.at[c], up_buf.at[c], up_send.at[c], up_recv.at[c], {"rows": z + 1})

    def down_copy(c):
        return copy(
            down_out.at[c], down_buf.at[c], down_send.at[c], down_recv.at[c], {"rows": z - 1}
        )

    def gr_copy(dest, slot):
        return copy(
            gram_own, gram_rows.at[slot], gr_send.at[dest], gr_recv.at[slot], {"rows": dest}
        )

    def gb_copy(dest, slot):
        return copy(
            gram_line, gram_blk.at[slot], gb_send.at[dest], gb_recv.at[slot], {"blk": dest}
        )

    def bu_copy(c):
        chunk = basis.at[:, aligned(c, width)]
        return copy(chunk, chunk, bu_send.at[c], bu_recv.at[c], {"rows": z + 1})

    def bd_copy(c):
        chunk = basis.at[:, aligned(c, width)]
        return copy(chunk, chunk, bd_send.at[c], bd_recv.at[c], {"rows": z - 1})

    def forward(c):
        return lax.dot_general(
            basis[:, aligned(c, width)],
            dense[:, aligned(c, width)],
            (((1,), (1,)), ((), ())),
            preferred_element_type=F32,
        )

    def backward(c):
        return jnp.dot(half[...], dense[:, aligned(c, width)], preferred_element_type=F32)

    @pl.loop(0, ITERS)
    def _(it):
        part[...] = forward(z)
        for d in range(1, m):

            @pl.when(z - d >= 0)
            def _():
                c = z - d

                @pl.when(it > 0)
                def _():
                    bu_copy(c).wait_recv()

                    @pl.when(z + 1 < m)
                    def _():
                        bu_copy(c).start()

                part[...] += forward(c)

            @pl.when(z + d < m)
            def _():
                c = z + d

                @pl.when(it > 0)
                def _():
                    bd_copy(c).wait_recv()

                    @pl.when(z > 0)
                    def _():
                        bd_copy(c).start()

                part[...] += forward(c)

        @pl.loop(0, owners)
        def _(q):
            @pl.when(q != b)
            def _():
                rs_copy(q, b).start()

        @pl.when(b < owners)
        def _():
            own = part[:, aligned(b, span)]

            def add(d, acc):
                src = lax.rem(b + d, n)
                rs_copy(b, src).wait_recv()
                return acc + rs_buf[src]

            own = lax.fori_loop(1, n, add, own)
            half_own[...] = own.astype(BF16)

            @pl.loop(1, n)
            def _(d):
                ag_copy(lax.rem(b + d, n), b).start()

            half[:, aligned(b, span)] = half_own[...]

        @pl.loop(0, owners)
        def _(q):
            @pl.when(q != b)
            def _():
                ag_copy(b, q).wait_recv()
                rs_copy(q, b).wait_send()

        for k in range(m - 1):
            c = m - 1 - k

            @pl.when(c > z)
            def _():
                mine = backward(c)

                @pl.when(z > 0)
                def _():
                    up_copy(c).wait_recv()
                    up_out[c] = mine + up_buf[c]

                @pl.when(z == 0)
                def _():
                    up_out[c] = mine

                up_copy(c).start()

            e = k

            @pl.when(e < z)
            def _():
                mine = backward(e)

                @pl.when(z < m - 1)
                def _():
                    down_copy(e).wait_recv()
                    down_out[e] = mine + down_buf[e]

                @pl.when(z == m - 1)
                def _():
                    down_out[e] = mine

                down_copy(e).start()

        hess_own[...] = backward(z)

        @pl.when(z > 0)
        def _():
            up_copy(z).wait_recv()
            hess_own[...] += up_buf[z]

        @pl.when(z < m - 1)
        def _():
            down_copy(z).wait_recv()
            hess_own[...] += down_buf[z]

        @pl.when(it > 0)
        def _():
            for c in range(m):

                @pl.when(jnp.logical_and(c <= z, z + 1 < m))
                def _():
                    bu_copy(c).wait_send()

                @pl.when(jnp.logical_and(c >= z, z > 0))
                def _():
                    bd_copy(c).wait_send()

        hess = hess_own[...]
        gram = lax.dot_general(
            hess, hess, (((1,), (1,)), ((), ())), precision=HIGHEST, preferred_element_type=F32
        )
        fold = vectors // 2
        gram_own[...] = jnp.concatenate([gram[:fold], gram[fold:]], axis=1)

        @pl.loop(1, m)
        def _(d):
            gr_copy(lax.rem(z + d, m), z).start()

        def add_line(d, acc):
            src = lax.rem(z + d, m)
            gr_copy(z, src).wait_recv()
            return acc + gram_rows[src]

        gram_line[...] = lax.fori_loop(1, m, add_line, gram_own[...])

        @pl.loop(1, n)
        def _(d):
            gb_copy(lax.rem(b + d, n), b).start()

        def add_blk(d, acc):
            src = lax.rem(b + d, n)
            gb_copy(b, src).wait_recv()
            return acc + gram_blk[src]

        packed = lax.fori_loop(1, n, add_blk, gram_line[...])
        gram = jnp.concatenate([packed[:, :vectors], packed[:, vectors:]], axis=0) / total

        for c in range(m):

            @pl.when(c > z)
            def _():
                up_copy(c).wait_send()

            @pl.when(c < z)
            def _():
                down_copy(c).wait_send()

        @pl.loop(1, m)
        def _(d):
            gr_copy(lax.rem(z + d, m), z).wait_send()

        @pl.loop(1, n)
        def _(d):
            gb_copy(lax.rem(b + d, n), b).wait_send()

        @pl.when(b < owners)
        def _():
            @pl.loop(1, n)
            def _(d):
                ag_copy(lax.rem(b + d, n), b).wait_send()

        result = jnp.dot(
            inverse_factor(gram), hess_own[...], precision=HIGHEST, preferred_element_type=F32
        )
        basis[:, aligned(z, width)] = result.astype(BF16)

        @pl.when(it < ITERS - 1)
        def _():
            @pl.when(z + 1 < m)
            def _():
                bu_copy(z).start()

            @pl.when(z > 0)
            def _():
                bd_copy(z).start()

        out_ref[it] = result


def local(n, m, sens_tiles, start_basis, row_blocks, col_blocks, live_counts):
    slots, tile = sens_tiles.shape[0], sens_tiles.shape[2]
    vectors, cells = start_basis.shape
    data, width = RB * tile, cells // m
    span = data // min(n, RB)
    numbers = jnp.arange(slots, dtype=jnp.int32)
    places = row_blocks[:, 0] * CB + col_blocks[:, 0]
    hit = (places[None, :] == jnp.arange(RB * CB, dtype=jnp.int32)[:, None]) & (
        numbers < live_counts[0, 0]
    )[None, :]
    inv = jnp.min(jnp.where(hit, numbers[None, :], slots), axis=1)
    total = float(cells * n)
    dma = pltpu.SemaphoreType.DMA
    return pl.pallas_call(
        functools.partial(kernel, n, m, total),
        out_shape=jax.ShapeDtypeStruct((ITERS, vectors, width), F32),
        in_specs=[
            pl.BlockSpec(memory_space=pltpu.SMEM),
            pl.BlockSpec(memory_space=pl.ANY),
            pl.BlockSpec(memory_space=pltpu.VMEM),
        ],
        out_specs=pl.BlockSpec(memory_space=pltpu.VMEM),
        scratch_shapes=[
            pltpu.VMEM((slots + 1, tile, tile), BF16),
            pltpu.VMEM((data, cells), BF16),
            pltpu.VMEM((vectors, cells), BF16),
            pltpu.VMEM((vectors, data), F32),
            pltpu.VMEM((n, vectors, span), F32),
            pltpu.VMEM((vectors, span), BF16),
            pltpu.VMEM((vectors, data), BF16),
            pltpu.VMEM((vectors, width), F32),
            pltpu.VMEM((m, vectors, width), F32),
            pltpu.VMEM((m, vectors, width), F32),
            pltpu.VMEM((m, vectors, width), F32),
            pltpu.VMEM((m, vectors, width), F32),
            pltpu.VMEM((vectors // 2, vectors * 2), F32),
            pltpu.VMEM((m, vectors // 2, vectors * 2), F32),
            pltpu.VMEM((vectors // 2, vectors * 2), F32),
            pltpu.VMEM((n, vectors // 2, vectors * 2), F32),
            dma,
            dma((n,)),
            dma((n,)),
            dma((n,)),
            dma((n,)),
            dma((m,)),
            dma((m,)),
            dma((m,)),
            dma((m,)),
            dma((m,)),
            dma((m,)),
            dma((n,)),
            dma((n,)),
            dma((m,)),
            dma((m,)),
            dma((m,)),
            dma((m,)),
        ],
        compiler_params=pltpu.CompilerParams(
            collective_id=0, has_side_effects=True, vmem_limit_bytes=56 * 1024 * 1024
        ),
        name="subspace",
    )(inv, sens_tiles, start_basis)


def solution(mesh):
    in_specs = (
        P("blk", "rows", None),
        P(None, "blk"),
        P("blk", "rows"),
        P("blk", "rows"),
        P("blk", "rows"),
    )
    out_specs = P(None, None, ("blk", "rows"))
    return jax.shard_map(
        functools.partial(local, mesh.shape["blk"], mesh.shape["rows"]),
        mesh=mesh,
        in_specs=in_specs,
        out_specs=out_specs,
        check_vma=False,
    )
```

time: 663 us -> 270 us (0.41); the launches traced: 653 us -> 270 us
  Pallas kernels: 0 us -> 265 us
  blocking collectives: 201 us -> 0 us
  waiting for transfers between devices: 197 us -> 0 us
  matrix products: 151 us -> 0 us
  other arithmetic: 51.9 us -> 1.41 us
  local copies, waits for them, and re-layouts: 37.5 us -> 2.31 us
  between operations: 14.7 us -> 0.67 us
    pallas_call x0 -> x1, Pallas kernels: none -> 265 us  [local(): pl.pallas_call(functools.partial(kernel, n, m, total), out_shape=jax.Shap...]
    psum x8 -> x0, blocking collectives: 201 us -> none  [the longest x4 104 us: local(): image = lax.psum(partial_image, 'blk')]
    psum x4 -> x0, waiting for transfers between devices: 197 us -> none  [local(): hessian = lax.psum(partial_hessian, 'rows')]
    dot_general x20 -> x0, matrix products: 142 us -> none  [the longest x4 41.5 us: apply_forward(): jnp.einsum('kst,sit->ksi', picked, sens_tiles, preferred_element_type=jnp...]
    another operation x21 -> x0, other arithmetic: 49.3 us -> none  [the longest x12 26.1 us: factor_whole(): lower = jnp.linalg.cholesky(gram)]
    gather x8 -> x0, local copies, waits for them, and re-layouts: 24.2 us -> none  [the longest x4 12.1 us: apply_forward(): jnp.take(basis_now.reshape(vectors, CB, tile_size), col_slots, axis=1)]
    another operation x4 -> x0, matrix products: 9.06 us -> none  [factor_whole(): return jax.scipy.linalg.solve_triangular(lower, current, lower=True)]
    unnamed x22 -> x1, local copies, waits for them, and re-layouts: 9.83 us -> 2.31 us
  transfers between devices with their start and end apart: 4 -> 0, of which waited for: 4 -> 0; matrix products, arithmetic and copies ran while one was open for 0% -> 0% of each run, Pallas kernels for 0% -> 0%
where the time goes in v1:
time: 270 us
  Pallas kernels  265 us (98%)
    pallas_call x1, Pallas kernels, local(): pl.pallas_call(functools.partial(kernel, n, m, total), out_shape=jax.Shap...  265 us

profile of v1, /device:TPU:0, one launch (start us, length us, event | category | flops | bytes accessed | tf_op | source)
XLA Modules:
  0.0 269.5 jit_solution(17060157658182051331)
XLA Ops:
  0.7 0.7 multiply_add_fusion
  1.4 0.7 select_reduce_fusion.inv_ref
  2.1 265.1 %subspace.1 = f32[4,64,1024]{2,1,0:T(8,128)} custom-call(s32[256]{0:T(256)} %select_reduce_fusion.inv_ref, bf16[256,128,128]{2,1,0:T(8,128)(2,1)} %tiles_hbm.1, bf16[64,4096]{1,0:T(8,128)(2,1)} %start_ref.1), custom_call_target="tpu_custom_call" | custom-call | tf_op jit(solution)/shard_map/subspace/pallas_call | solution.py:401
  267.2 2.3 copy.8
  (1 shorter events, 0.0 us)

commit v2 on v1

--- a/solution.py
+++ b/solution.py
@@ -14,6 +14,9 @@
 F32 = jnp.float32
 BF16 = jnp.bfloat16
 HIGHEST = lax.Precision.HIGHEST
+CODE = jnp.int16
+TOP = 32767.0
+PIECES = 2
 
 
 def aligned(index, width):
@@ -43,6 +46,27 @@
     return whole[:, size:] * (1.0 / jnp.sqrt(pivots))
 
 
+def diagonal_of(size):
+    row_id = lax.broadcasted_iota(jnp.int32, (size, size), 0)
+    return row_id == lax.broadcasted_iota(jnp.int32, (size, size), 1)
+
+
+def encode(values, code_ref, scale_ref):
+    size = values.shape[0]
+    top = jnp.maximum(jnp.max(jnp.abs(values), axis=1, keepdims=True), 1e-30)
+    code_ref[...] = jnp.round(values * (TOP / top)).astype(jnp.int32).astype(CODE)
+    along = jnp.sum(jnp.where(diagonal_of(size), top * (1.0 / TOP), 0.0), axis=0, keepdims=True)
+    scale_ref[:, :size] = jnp.broadcast_to(along, (8, size))
+    scale_ref[:, size:] = jnp.broadcast_to(along, (8, size))
+
+
+def decode(code_ref, scale_ref):
+    size = code_ref.shape[0]
+    along = scale_ref[0:1, :size]
+    scale = jnp.sum(jnp.where(diagonal_of(size), along, 0.0), axis=1, keepdims=True)
+    return code_ref[...].astype(F32) * scale
+
+
 def kernel(
     n,
     m,
@@ -63,6 +87,12 @@
     up_buf,
     down_out,
     down_buf,
+    up_out_scale,
+    up_scale,
+    down_out_scale,
+    down_scale,
+    up_sum,
+    down_sum,
     gram_own,
     gram_rows,
     gram_line,
@@ -84,6 +114,10 @@
     bu_recv,
     bd_send,
     bd_recv,
+    us_send,
+    us_recv,
+    ds_send,
+    ds_recv,
 ):
     slots = tiles_hbm.shape[0]
     tile = tiles_hbm.shape[1]
@@ -153,13 +187,31 @@
             {"blk": dest},
         )
 
-    def up_copy(c):
-        return copy(up_out.at[c], up_buf.at[c], up_send.at[c], up_recv.at[c], {"rows": z + 1})
-
-    def down_copy(c):
-        return copy(
-            down_out.at[c], down_buf.at[c], down_send.at[c], down_recv.at[c], {"rows": z - 1}
-        )
+    def up_copies(c):
+        there = {"rows": z + 1}
+        return (
+            copy(up_out_scale.at[c], up_scale.at[c], us_send.at[c], us_recv.at[c], there),
+            copy(up_out.at[c], up_buf.at[c], up_send.at[c], up_recv.at[c], there),
+        )
+
+    def down_copies(c):
+        there = {"rows": z - 1}
+        return (
+            copy(down_out_scale.at[c], down_scale.at[c], ds_send.at[c], ds_recv.at[c], there),
+            copy(down_out.at[c], down_buf.at[c], down_send.at[c], down_recv.at[c], there),
+        )
+
+    def start(copies):
+        for each in copies:
+            each.start()
+
+    def wait_recv(copies):
+        for each in copies:
+            each.wait_recv()
+
+    def wait_send(copies):
+        for each in copies:
+            each.wait_send()
 
     def gr_copy(dest, slot):
         return copy(
@@ -171,13 +223,17 @@
             gram_line, gram_blk.at[slot], gb_send.at[dest], gb_recv.at[slot], {"blk": dest}
         )
 
-    def bu_copy(c):
-        chunk = basis.at[:, aligned(c, width)]
-        return copy(chunk, chunk, bu_send.at[c], bu_recv.at[c], {"rows": z + 1})
-
-    def bd_copy(c):
-        chunk = basis.at[:, aligned(c, width)]
-        return copy(chunk, chunk, bd_send.at[c], bd_recv.at[c], {"rows": z - 1})
+    piece = width // PIECES
+
+    def bu_copy(c, p):
+        k = c * PIECES + p
+        chunk = basis.at[:, aligned(k, piece)]
+        return copy(chunk, chunk, bu_send.at[k], bu_recv.at[k], {"rows": z + 1})
+
+    def bd_copy(c, p):
+        k = c * PIECES + p
+        chunk = basis.at[:, aligned(k, piece)]
+        return copy(chunk, chunk, bd_send.at[k], bd_recv.at[k], {"rows": z - 1})
 
     def forward(c):
         return lax.dot_general(
@@ -194,34 +250,31 @@
     def _(it):
         part[...] = forward(z)
         for d in range(1, m):
-
-            @pl.when(z - d >= 0)
-            def _():
-                c = z - d
-
-                @pl.when(it > 0)
+            for p in range(PIECES):
+
+                @pl.when(jnp.logical_and(it > 0, z - d >= 0))
                 def _():
-                    bu_copy(c).wait_recv()
+                    bu_copy(z - d, p).wait_recv()
 
                     @pl.when(z + 1 < m)
                     def _():
-                        bu_copy(c).start()
-
-                part[...] += forward(c)
-
-            @pl.when(z + d < m)
-            def _():
-                c = z + d
-
-                @pl.when(it > 0)
+                        bu_copy(z - d, p).start()
+
+                @pl.when(jnp.logical_and(it > 0, z + d < m))
                 def _():
-                    bd_copy(c).wait_recv()
+                    bd_copy(z + d, p).wait_recv()
 
                     @pl.when(z > 0)
                     def _():
-                        bd_copy(c).start()
-
-                part[...] += forward(c)
+                        bd_copy(z + d, p).start()
+
+            @pl.when(z - d >= 0)
+            def _():
+                part[...] += forward(z - d)
+
+            @pl.when(z + d < m)
+            def _():
+                part[...] += forward(z + d)
 
         @pl.loop(0, owners)
         def _(q):
@@ -259,59 +312,54 @@
 
             @pl.when(c > z)
             def _():
-                mine = backward(c)
+                up_sum[...] = backward(c)
 
                 @pl.when(z > 0)
                 def _():
-                    up_copy(c).wait_recv()
-                    up_out[c] = mine + up_buf[c]
-
-                @pl.when(z == 0)
-                def _():
-                    up_out[c] = mine
-
-                up_copy(c).start()
+                    wait_recv(up_copies(c))
+                    up_sum[...] += decode(up_buf.at[c], up_scale.at[c])
+
+                encode(up_sum[...], up_out.at[c], up_out_scale.at[c])
+                start(up_copies(c))
 
             e = k
 
             @pl.when(e < z)
             def _():
-                mine = backward(e)
+                down_sum[...] = backward(e)
 
                 @pl.when(z < m - 1)
                 def _():
-                    down_copy(e).wait_recv()
-                    down_out[e] = mine + down_buf[e]
-
-                @pl.when(z == m - 1)
-                def _():
-                    down_out[e] = mine
-
-                down_copy(e).start()
+                    wait_recv(down_copies(e))
+                    down_sum[...] += decode(down_buf.at[e], down_scale.at[e])
+
+                encode(down_sum[...], down_out.at[e], down_out_scale.at[e])
+                start(down_copies(e))
 
         hess_own[...] = backward(z)
 
         @pl.when(z > 0)
         def _():
-            up_copy(z).wait_recv()
-            hess_own[...] += up_buf[z]
+            wait_recv(up_copies(z))
+            hess_own[...] += decode(up_buf.at[z], up_scale.at[z])
 
         @pl.when(z < m - 1)
         def _():
-            down_copy(z).wait_recv()
-            hess_own[...] += down_buf[z]
+            wait_recv(down_copies(z))
+            hess_own[...] += decode(down_buf.at[z], down_scale.at[z])
 
         @pl.when(it > 0)
         def _():
             for c in range(m):
-
-                @pl.when(jnp.logical_and(c <= z, z + 1 < m))
-                def _():
-                    bu_copy(c).wait_send()
-
-                @pl.when(jnp.logical_and(c >= z, z > 0))
-                def _():
-                    bd_copy(c).wait_send()
+                for p in range(PIECES):
+
+                    @pl.when(jnp.logical_and(c <= z, z + 1 < m))
+                    def _():
+                        bu_copy(c, p).wait_send()
+
+                    @pl.when(jnp.logical_and(c >= z, z > 0))
+                    def _():
+                        bd_copy(c, p).wait_send()
 
         hess = hess_own[...]
         gram = lax.dot_general(
@@ -347,11 +395,11 @@
 
             @pl.when(c > z)
             def _():
-                up_copy(c).wait_send()
+                wait_send(up_copies(c))
 
             @pl.when(c < z)
             def _():
-                down_copy(c).wait_send()
+                wait_send(down_copies(c))
 
         @pl.loop(1, m)
         def _(d):
@@ -374,13 +422,15 @@
 
         @pl.when(it < ITERS - 1)
         def _():
-            @pl.when(z + 1 < m)
-            def _():
-                bu_copy(z).start()
-
-            @pl.when(z > 0)
-            def _():
-                bd_copy(z).start()
+            for p in range(PIECES):
+
+                @pl.when(z + 1 < m)
+                def _():
+                    bu_copy(z, p).start()
+
+                @pl.when(z > 0)
+                def _():
+                    bd_copy(z, p).start()
 
         out_ref[it] = result
 
@@ -416,10 +466,16 @@
             pltpu.VMEM((vectors, span), BF16),
             pltpu.VMEM((vectors, data), BF16),
             pltpu.VMEM((vectors, width), F32),
-            pltpu.VMEM((m, vectors, width), F32),
-            pltpu.VMEM((m, vectors, width), F32),
-            pltpu.VMEM((m, vectors, width), F32),
-            pltpu.VMEM((m, vectors, width), F32),
+            pltpu.VMEM((m, vectors, width), CODE),
+            pltpu.VMEM((m, vectors, width), CODE),
+            pltpu.VMEM((m, vectors, width), CODE),
+            pltpu.VMEM((m, vectors, width), CODE),
+            pltpu.VMEM((m, 8, vectors * 2), F32),
+            pltpu.VMEM((m, 8, vectors * 2), F32),
+            pltpu.VMEM((m, 8, vectors * 2), F32),
+            pltpu.VMEM((m, 8, vectors * 2), F32),
+            pltpu.VMEM((vectors, width), F32),
+            pltpu.VMEM((vectors, width), F32),
             pltpu.VMEM((vectors // 2, vectors * 2), F32),
             pltpu.VMEM((m, vectors // 2, vectors * 2), F32),
             pltpu.VMEM((vectors // 2, vectors * 2), F32),
@@ -437,6 +493,10 @@
             dma((m,)),
             dma((n,)),
             dma((n,)),
+            dma((m * PIECES,)),
+            dma((m * PIECES,)),
+            dma((m * PIECES,)),
+            dma((m * PIECES,)),
             dma((m,)),
             dma((m,)),
             dma((m,)),

time: 270 us -> 229 us (0.85)
  Pallas kernels: 265 us -> 224 us
    pallas_call x1, Pallas kernels: 265 us -> 224 us  [local(): pl.pallas_call(functools.partial(kernel, n, m, total), out_shape=jax.Shap...]
where the time goes in v2:
time: 229 us; the launch traced here: 228 us
  Pallas kernels  224 us (98%)
  local copies, waits for them, and re-layouts  2.31 us (1%)
    pallas_call x1, Pallas kernels, local(): pl.pallas_call(functools.partial(kernel, n, m, total), out_shape=jax.Shap...  224 us

profile of v2, /device:TPU:0, one launch (start us, length us, event | category | flops | bytes accessed | tf_op | source)
XLA Modules:
  0.0 228.4 jit_solution(8714058162745930986)
XLA Ops:
  0.7 0.7 multiply_add_fusion
  1.4 0.7 select_reduce_fusion.inv_ref
  2.1 224.0 %subspace.1 = f32[4,64,1024]{2,1,0:T(8,128)} custom-call(s32[256]{0:T(256)} %select_reduce_fusion.inv_ref, bf16[256,128,128]{2,1,0:T(8,128)(2,1)} %tiles_hbm.1, bf16[64,4096]{1,0:T(8,128)(2,1)} %start_ref.1), custom_call_target="tpu_custom_call" | custom-call | tf_op jit(solution)/shard_map/subspace/pallas_call | solution.py:451
  226.1 2.3 %copy.8 = f32[4,64,1024]{2,1,0:T(8,128)} copy(f32[4,64,1024]{2,1,0:T(8,128)} %subspace.1) | data formatting | bytes 2097152
  (1 shorter events, 0.0 us)

commit v3 on v2

--- a/solution.py
+++ b/solution.py
@@ -17,6 +17,7 @@
 CODE = jnp.int16
 TOP = 32767.0
 PIECES = 2
+SPLIT = 2
 
 
 def aligned(index, width):
@@ -29,18 +30,40 @@
     lane_id = lax.broadcasted_iota(jnp.int32, (size, size), 1)
     eye = (row_id == lane_id).astype(F32)
     whole = jnp.concatenate([gram, eye], axis=1)
-    step = 8
-    blocks = [whole[b * step : (b + 1) * step, :] for b in range(size // step)]
-    sub_id = lax.broadcasted_iota(jnp.int32, (step, 2 * size), 0)
-    for j in range(size):
-        home, within = divmod(j, step)
-        row = blocks[home][within : within + 1, :]
-        scaled = row / row[:, j : j + 1]
-        for b in range(home, size // step):
-            update = blocks[b][:, j : j + 1] * scaled
-            if b == home:
-                update = jnp.where(sub_id > within, update, 0.0)
-            blocks[b] = blocks[b] - update
+    step, group = 8, 4
+    lanes = 2 * size
+    blocks = [whole[k * step : (k + 1) * step, :] for k in range(size // step)]
+    sub_id = lax.broadcasted_iota(jnp.int32, (step, lanes), 0)
+    for first in range(0, size, group):
+        home, within = divmod(first, step)
+        rows = [blocks[home][within + g : within + g + 1, :] for g in range(group)]
+        entry = [
+            [jnp.broadcast_to(row[:, first + g : first + g + 1], (1, lanes)) for g in range(group)]
+            for row in rows
+        ]
+        columns = {
+            k: [
+                jnp.broadcast_to(blocks[k][:, first + g : first + g + 1], (step, lanes))
+                for g in range(group)
+            ]
+            for k in range(home, size // step)
+        }
+        for g in range(group):
+            over = 1.0 / entry[g][g]
+            scaled = rows[g] * over
+            ratio = [entry[g][h] * over for h in range(group)]
+            for k in range(home, size // step):
+                column = columns[k][g]
+                if k == home:
+                    column = jnp.where(sub_id > within + g, column, 0.0)
+                blocks[k] = blocks[k] - column * scaled
+                for h in range(g + 1, group):
+                    columns[k][h] = columns[k][h] - column * ratio[h]
+            for low in range(g + 1, group):
+                factor = entry[low][g]
+                rows[low] = rows[low] - factor * scaled
+                for h in range(g + 1, group):
+                    entry[low][h] = entry[low][h] - factor * ratio[h]
     whole = jnp.concatenate(blocks, axis=0)
     pivots = jnp.sum(whole[:, :size] * eye, axis=1, keepdims=True)
     return whole[:, size:] * (1.0 / jnp.sqrt(pivots))
@@ -224,6 +247,7 @@
         )
 
     piece = width // PIECES
+    strip = width // SPLIT
 
     def bu_copy(c, p):
         k = c * PIECES + p
@@ -243,8 +267,8 @@
             preferred_element_type=F32,
         )
 
-    def backward(c):
-        return jnp.dot(half[...], dense[:, aligned(c, width)], preferred_element_type=F32)
+    def backward(k):
+        return jnp.dot(half[...], dense[:, aligned(k, strip)], preferred_element_type=F32)
 
     @pl.loop(0, ITERS)
     def _(it):
@@ -310,43 +334,50 @@
         for k in range(m - 1):
             c = m - 1 - k
 
-            @pl.when(c > z)
-            def _():
-                up_sum[...] = backward(c)
-
-                @pl.when(z > 0)
+            e = k
+            for p in range(SPLIT):
+                j = c * SPLIT + p
+
+                @pl.when(c > z)
                 def _():
-                    wait_recv(up_copies(c))
-                    up_sum[...] += decode(up_buf.at[c], up_scale.at[c])
-
-                encode(up_sum[...], up_out.at[c], up_out_scale.at[c])
-                start(up_copies(c))
-
-            e = k
-
-            @pl.when(e < z)
-            def _():
-                down_sum[...] = backward(e)
-
-                @pl.when(z < m - 1)
+                    up_sum[...] = backward(j)
+
+                    @pl.when(z > 0)
+                    def _():
+                        wait_recv(up_copies(j))
+                        up_sum[...] += decode(up_buf.at[j], up_scale.at[j])
+
+                    encode(up_sum[...], up_out.at[j], up_out_scale.at[j])
+                    start(up_copies(j))
+
+                i = e * SPLIT + p
+
+                @pl.when(e < z)
                 def _():
-                    wait_recv(down_copies(e))
-                    down_sum[...] += decode(down_buf.at[e], down_scale.at[e])
-
-                encode(down_sum[...], down_out.at[e], down_out_scale.at[e])
-                start(down_copies(e))
-
-        hess_own[...] = backward(z)
-
-        @pl.when(z > 0)
-        def _():
-            wait_recv(up_copies(z))
-            hess_own[...] += decode(up_buf.at[z], up_scale.at[z])
-
-        @pl.when(z < m - 1)
-        def _():
-            wait_recv(down_copies(z))
-            hess_own[...] += decode(down_buf.at[z], down_scale.at[z])
+                    down_sum[...] = backward(i)
+
+                    @pl.when(z < m - 1)
+                    def _():
+                        wait_recv(down_copies(i))
+                        down_sum[...] += decode(down_buf.at[i], down_scale.at[i])
+
+                    encode(down_sum[...], down_out.at[i], down_out_scale.at[i])
+                    start(down_copies(i))
+
+        for p in range(SPLIT):
+            own = slice(p * strip, (p + 1) * strip)
+            j = z * SPLIT + p
+            hess_own[:, own] = backward(j)
+
+            @pl.when(z > 0)
+            def _():
+                wait_recv(up_copies(j))
+                hess_own[:, own] += decode(up_buf.at[j], up_scale.at[j])
+
+            @pl.when(z < m - 1)
+            def _():
+                wait_recv(down_copies(j))
+                hess_own[:, own] += decode(down_buf.at[j], down_scale.at[j])
 
         @pl.when(it > 0)
         def _():
@@ -395,11 +426,13 @@
 
             @pl.when(c > z)
             def _():
-                wait_send(up_copies(c))
+                for p in range(SPLIT):
+                    wait_send(up_copies(c * SPLIT + p))
 
             @pl.when(c < z)
             def _():
-                wait_send(down_copies(c))
+                for p in range(SPLIT):
+                    wait_send(down_copies(c * SPLIT + p))
 
         @pl.loop(1, m)
         def _(d):
@@ -466,16 +499,16 @@
             pltpu.VMEM((vectors, span), BF16),
             pltpu.VMEM((vectors, data), BF16),
             pltpu.VMEM((vectors, width), F32),
-            pltpu.VMEM((m, vectors, width), CODE),
-            pltpu.VMEM((m, vectors, width), CODE),
-            pltpu.VMEM((m, vectors, width), CODE),
-            pltpu.VMEM((m, vectors, width), CODE),
-            pltpu.VMEM((m, 8, vectors * 2), F32),
-            pltpu.VMEM((m, 8, vectors * 2), F32),
-            pltpu.VMEM((m, 8, vectors * 2), F32),
-            pltpu.VMEM((m, 8, vectors * 2), F32),
-            pltpu.VMEM((vectors, width), F32),
-            pltpu.VMEM((vectors, width), F32),
+            pltpu.VMEM((m * SPLIT, vectors, width // SPLIT), CODE),
+            pltpu.VMEM((m * SPLIT, vectors, width // SPLIT), CODE),
+            pltpu.VMEM((m * SPLIT, vectors, width // SPLIT), CODE),
+            pltpu.VMEM((m * SPLIT, vectors, width // SPLIT), CODE),
+            pltpu.VMEM((m * SPLIT, 8, vectors * 2), F32),
+            pltpu.VMEM((m * SPLIT, 8, vectors * 2), F32),
+            pltpu.VMEM((m * SPLIT, 8, vectors * 2), F32),
+            pltpu.VMEM((m * SPLIT, 8, vectors * 2), F32),
+            pltpu.VMEM((vectors, width // SPLIT), F32),
+            pltpu.VMEM((vectors, width // SPLIT), F32),
             pltpu.VMEM((vectors // 2, vectors * 2), F32),
             pltpu.VMEM((m, vectors // 2, vectors * 2), F32),
             pltpu.VMEM((vectors // 2, vectors * 2), F32),
@@ -485,10 +518,10 @@
             dma((n,)),
             dma((n,)),
             dma((n,)),
-            dma((m,)),
-            dma((m,)),
-            dma((m,)),
-            dma((m,)),
+            dma((m * SPLIT,)),
+            dma((m * SPLIT,)),
+            dma((m * SPLIT,)),
+            dma((m * SPLIT,)),
             dma((m,)),
             dma((m,)),
             dma((n,)),
@@ -497,10 +530,10 @@
             dma((m * PIECES,)),
             dma((m * PIECES,)),
             dma((m * PIECES,)),
-            dma((m,)),
-            dma((m,)),
-            dma((m,)),
-            dma((m,)),
+            dma((m * SPLIT,)),
+            dma((m * SPLIT,)),
+            dma((m * SPLIT,)),
+            dma((m * SPLIT,)),
         ],
         compiler_params=pltpu.CompilerParams(
             collective_id=0, has_side_effects=True, vmem_limit_bytes=56 * 1024 * 1024

time: 229 us -> 230 us (level)
  no operation moved by 1% of the time
where the time goes in v3:
time: 230 us
  Pallas kernels  226 us (98%)
  local copies, waits for them, and re-layouts  2.31 us (1%)
    pallas_call x1, Pallas kernels, local(): pl.pallas_call(functools.partial(kernel, n, m, total), out_shape=jax.Shap...  226 us

profile of v3, /device:TPU:0, one launch (start us, length us, event | category | flops | bytes accessed | tf_op | source)
XLA Modules:
  0.0 230.1 jit_solution(4873994783439312684)
XLA Ops:
  0.7 0.7 multiply_add_fusion
  1.4 0.7 select_reduce_fusion.inv_ref
  2.1 225.7 %subspace.1 = f32[4,64,1024]{2,1,0:T(8,128)} custom-call(s32[256]{0:T(256)} %select_reduce_fusion.inv_ref, bf16[256,128,128]{2,1,0:T(8,128)(2,1)} %tiles_hbm.1, bf16[64,4096]{1,0:T(8,128)(2,1)} %start_ref.1), custom_call_target="tpu_custom_call" | custom-call | tf_op jit(solution)/shard_map/subspace/pallas_call | solution.py:484
  227.8 2.3 %copy.8 = f32[4,64,1024]{2,1,0:T(8,128)} copy(f32[4,64,1024]{2,1,0:T(8,128)} %subspace.1) | data formatting | bytes 2097152
  (1 shorter events, 0.0 us)
